TPU v7x, 32 devices: a whole 2x2x4 slice. The times are simulated.
32 devices in a mesh: dp: 8 (over z, y), col: 4 (over x, core).
Axes of the slice: x: 2, y: 2, z: 4, core: 2. Of those that a mesh axis runs over, the one named last changes fastest.
Arguments:
- tokens: bfloat16 [8192, 8192], P('dp', 'col'), may hold values from -6 to 6
- out_grad: bfloat16 [8192, 8192], P(('dp', 'col')), may hold values from -6 to 6
- weight: float32 [8192, 8192], P('dp', 'col'), may hold values from -6 to 6
- second: float32 [8192, 8192], P('dp', 'col'), may hold values from 0.0001 to 0.001
- momentum: float32 [8192, 512], P(('dp', 'col')), may hold values from -0.12 to 0.12
- sign_seed: int32 [1], replicated, may hold values from 0 to 999999
- step_number: int32 [1], replicated, may hold values from 1 to 999999
Outputs:
- new_weight: float32 [8192, 8192], P('dp', 'col')
- new_second: float32 [8192, 8192], P('dp', 'col')
- new_momentum: float32 [8192, 512], P(('dp', 'col'))
All inputs are finite; a program needn't handle non-finite values.
Results may differ from a plain program's by a relative error of at most 0.00097.
Values may be sent and summed in bfloat16 or wider, within the bound.
No kernel may reach another device: no remote copies, remote signals or barrier semaphores. Data moves between devices by JAX's collectives and lax.ppermute only.
A program may use at most 128 MiB of HBM per device.

v0:
```python
import jax
import jax.numpy as jnp
from jax import lax
from jax.sharding import PartitionSpec as P


def sign_table(sign_seed, step_number, first_row, row_count, low_rank):
    row_ids = first_row + lax.iota(jnp.int32, row_count)
    col_ids = lax.iota(jnp.int32, low_rank)
    flat_index = row_ids[:, None] * low_rank + col_ids[None, :]
    hashed = flat_index * 747796405 + sign_seed[0] * 1664525 + step_number[0] * 1013904223
    hashed = hashed ^ hashed >> 16 & 65535
    hashed = hashed * 2127912213
    hashed = hashed ^ hashed >> 13 & 524287
    hashed = hashed * 1103515245
    hashed = hashed ^ hashed >> 16 & 65535
    low_bit = hashed >> 20 & 1
    return (1 - 2 * low_bit).astype(jnp.float32)


def contract(left_rows, right_rows):
    return lax.dot_general(
        left_rows, right_rows, (((0,), (0,)), ((), ())), preferred_element_type=jnp.float32
    )


def per_device(tokens, out_grad, weight, second, momentum, sign_seed, step_number):
    local_tokens, din_local = tokens.shape
    low_rank = momentum.shape[1]
    owner_rows = momentum.shape[0]
    inv_root = 1.0 / jnp.sqrt(jnp.float32(low_rank))
    col_position = lax.axis_index("col")
    sign_block = sign_table(sign_seed, step_number, col_position * din_local, din_local, low_rank)
    partial_sketch = (
        jnp.dot(tokens, sign_block.astype(jnp.bfloat16), preferred_element_type=jnp.float32)
        * inv_root
    )
    quarter = lax.psum_scatter(partial_sketch, "col", scatter_dimension=0, tiled=True)
    sketch = quarter.astype(jnp.bfloat16)
    total_tokens = lax.axis_size("dp") * local_tokens
    data_count = lax.axis_size("dp")
    col_count = lax.axis_size("col")
    quarter_rows = out_grad.shape[0]
    grouped = out_grad.reshape(quarter_rows, data_count, col_count, owner_rows)
    grouped = jnp.transpose(grouped, (0, 2, 1, 3)).reshape(
        quarter_rows, col_count, data_count * owner_rows
    )
    regrouped = lax.all_to_all(grouped, "col", split_axis=1, concat_axis=0, tiled=True)
    regrouped = regrouped.reshape(quarter_rows * col_count, data_count * owner_rows)
    shard_sketch = lax.all_gather(sketch, "col", axis=0, tiled=True)
    projected = lax.psum_scatter(
        contract(regrouped, shard_sketch), "dp", scatter_dimension=0, tiled=True
    )
    projected = projected / jnp.float32(total_tokens)
    new_momentum = 0.8 * momentum + 0.2 * projected
    row_block = lax.all_gather(new_momentum, "col", axis=0, tiled=True)
    dense_grad = (
        lax.dot_general(
            row_block,
            sign_block,
            (((1,), (1,)), ((), ())),
            precision=lax.Precision.HIGHEST,
            preferred_element_type=jnp.float32,
        )
        * inv_root
    )
    new_second = 0.95 * second + 0.05 * dense_grad * dense_grad
    new_weight = weight - 0.5 * dense_grad / (jnp.sqrt(new_second) + 1e-08)
    return (new_weight, new_second, new_momentum)


def solution(mesh):
    placed = (
        P("dp", "col"),
        P(("dp", "col"), None),
        P("dp", "col"),
        P("dp", "col"),
        P(("dp", "col"), None),
        P(),
        P(),
    )
    return jax.shard_map(
        per_device,
        mesh=mesh,
        in_specs=placed,
        out_specs=(P("dp", "col"), P("dp", "col"), P(("dp", "col"), None)),
        check_vma=False,
    )
```

profile of v0, /device:TPU:0, one launch (start us, length us, event | category | flops | bytes accessed | tf_op | source)
XLA Modules:
  0.0 263.5 jit_solution(1373859997120523536)
XLA Ops:
  7.2 0.0 reduce-scatter.3.cloned.1.call-start
  8.5 7.7 %multiply_bitcast_fusion = f32[1024,512]{0,1:T(8,128)} fusion(bf16[1024,2048]{1,0:T(8,128)(2,1)} %param.7, s32[]{:T(128)} %bitcast.1, s32[]{:T(128)} %bitcast, s32[2048]{0:T(1024)S(1)} %add_multiply_fusion), kind=kOutput, calls=%fused_computation.9 | convolution fusion | flops 2170028032 | bytes 6299656 | tf_op jit(solution)/shard_map/dot_general | solution.py:35
  16.2 0.0 reduce-scatter.3.cloned.1.call-update
  16.3 7.8 %reshape.26 = bf16[256,8,4,256]{3,2,1,0:T(4,128)(2,1)} reshape(bf16[256,8192]{1,0:T(8,128)(2,1)} %param.8) | data formatting | bytes 8388608 | tf_op jit(solution)/shard_map/reshape | solution.py:44
  24.1 4.9 %copy.16 = bf16[256,8,4,256]{3,1,0,2:T(8,128)(2,1)} copy(bf16[256,8,4,256]{3,2,1,0:T(4,128)(2,1)} %reshape.26) | data formatting | bytes 8388608 | tf_op jit(solution)/shard_map/reshape | solution.py:44
  29.0 7.4 %reshape.27 = bf16[256,4,2048]{2,0,1:T(8,128)(2,1)} reshape(bf16[256,4,8,256]{3,2,0,1:T(8,128)(2,1)} %bitcast.22) | data formatting | bytes 8388608 | tf_op jit(solution)/shard_map/reshape | solution.py:45
  36.3 4.8 %all-to-all-start = ((bf16[256,4,2048]{2,0,1:T(8,128)(2,1)}), bf16[256,4,2048]{2,0,1:T(8,128)(2,1)}, u32[]{:S(2)}, u32[]{:S(2)}) async-start(bf16[256,4,2048]{2,0,1:T(8,128)(2,1)} %reshape.27), calls=%async_computation.1 | async-start | bytes 8388608 | tf_op jit(solution)/shard_map/all_to_all | solution.py:48
  41.2 0.0 all-gather.3.cloned.1.call-start
  41.2 12.6 %reduce-scatter.3.cloned.1.call-done = f32[256,512]{0,1:T(8,128)} async-done(((f32[1024,512]{0,1:T(8,128)}), f32[256,512]{0,1:T(8,128)}) %reduce-scatter.3.cloned.1.call-update) | async-done | bytes 524304 | tf_op jit(solution)/shard_map/reduce_scatter | solution.py:38
  53.8 1.8 convert_element_type.11
  55.6 0.0 all-gather.3.cloned.1.call-update
  55.6 0.0 reduce-scatter.5.cloned.1.call-start
  55.7 44.1 %all-to-all-done = bf16[256,4,2048]{2,0,1:T(8,128)(2,1)} async-done(((bf16[256,4,2048]{2,0,1:T(8,128)(2,1)}), bf16[256,4,2048]{2,0,1:T(8,128)(2,1)}, u32[]{:S(2)}, u32[]{:S(2)}) %all-to-all-start) | async-done | bytes 4194336 | tf_op jit(solution)/shard_map/all_to_all | solution.py:48
  99.7 0.0 all-gather.3.cloned.1.call-done
  99.7 6.9 %convolution_bitcast_fusion = f32[2048,512]{0,1:T(8,128)} fusion(bf16[1024,512]{0,1:T(8,128)(2,1)} %all-gather.3.cloned.1.call-done, bf16[1024,2048]{1,0:T(8,128)(2,1)} %bitcast.6), kind=kOutput, calls=%fused_computation.7 | convolution fusion | flops 2147483648 | bytes 9437184 | tf_op jit(solution)/shard_map/dot_general | solution.py:22
  106.6 0.0 copy-start
  106.6 0.0 reduce-scatter.5.cloned.1.call-update
  106.6 0.2 all-gather.5.cloned.1.call-start
  106.9 0.8 copy-done
  107.6 0.2 copy.12
  107.8 87.7 %reduce-scatter.5.cloned.1.call-done = f32[256,512]{0,1:T(8,128)} async-done(((f32[2048,512]{0,1:T(8,128)}), f32[256,512]{0,1:T(8,128)}) %reduce-scatter.5.cloned.1.call-update) | async-done | bytes 524304 | tf_op jit(solution)/shard_map/reduce_scatter | solution.py:51
  195.5 1.9 multiply_add_fusion.1
  197.5 0.0 all-gather.5.cloned.1.call-update
  197.5 2.0 copy.14
  199.5 20.3 %all-gather.5.cloned.1.call-done = f32[1024,512]{0,1:T(8,128)} async-done(((f32[256,512]{0,1:T(8,128)}), f32[1024,512]{0,1:T(8,128)}) %all-gather.5.cloned.1.call-update) | async-done | bytes 2097168 | tf_op jit(solution)/shard_map/all_gather | solution.py:56
  219.8 37.1 %divide_subtract_fusion = (f32[1024,2048]{1,0:T(8,128)}, f32[1024,2048]{1,0:T(8,128)}) fusion(f32[1024,2048]{1,0:T(8,128)} %param.9, f32[1024,2048]{1,0:T(8,128)} %param.10, f32[1024,512]{0,1:T(8,128)} %all-gather.5.cloned.1.call-done, s32[]{:T(128)} %bitcast.1, s32[]{:T(128)} %bitcast, s32[2048]{0:T(1024)S(1)} %add_multiply_fusion), kind=kOutput, calls=%fused_computation | convolution fusion | flops 12924747776 | bytes 35659784 | tf_op jit(solution)/shard_map/dot_general | solution.py:58
  (1 shorter events, 0.0 us)
Async XLA Ops:
  7.2 46.7 %reduce-scatter.3.cloned.1.call-start = ((), (), s32[]{:S(2)}) async-start(), calls=%async_computation.3 | async-start | bytes 2621440 | tf_op jit(solution)/shard_map/reduce_scatter | solution.py:38
  36.3 63.4 %all-to-all-start = ((bf16[256,4,2048]{2,0,1:T(8,128)(2,1)}), bf16[256,4,2048]{2,0,1:T(8,128)(2,1)}, u32[]{:S(2)}, u32[]{:S(2)}) async-start(bf16[256,4,2048]{2,0,1:T(8,128)(2,1)} %reshape.27), calls=%async_computation.1 | async-start | bytes 8388608 | tf_op jit(solution)/shard_map/all_to_all | solution.py:48
  41.2 58.5 %all-gather.3.cloned.1.call-start = ((), (), s32[]{:S(2)}) async-start(), calls=%async_computation.4 | async-start | bytes 1310720 | tf_op jit(solution)/shard_map/all_gather | solution.py:50
  55.6 139.9 %reduce-scatter.5.cloned.1.call-start = ((), (), s32[]{:S(2)}) async-start(), calls=%async_computation.5 | async-start | bytes 4718592 | tf_op jit(solution)/shard_map/reduce_scatter | solution.py:51
  106.6 1.0 copy-start
  106.6 113.2 %all-gather.5.cloned.1.call-start = ((), (), s32[]{:S(2)}) async-start(), calls=%async_computation.6 | async-start | bytes 2621440 | tf_op jit(solution)/shard_map/all_gather | solution.py:56
Sparse Core Ops, SparseCore 0:
  16.4 37.4 reduce-scatter.2
  56.0 21.9 all-gather.2
  106.7 88.7 reduce-scatter.4
  197.6 22.1 all-gather.4
where the time goes:
time: 264 us; the launch traced here: 263 us
  waiting for transfers between devices  165 us (62%)
  matrix products  51.7 us (20%)
  local copies, waits for them, and re-layouts  23.1 us (9%)
  between operations  15.1 us (6%)
  starting transfers between devices  5.19 us (2%)
  other arithmetic  3.69 us (1%)
    reduce_scatter x1, waiting for transfers between devices, per_device(): lax.psum_scatter(contract(regrouped, shard_sketch), 'dp', scatter_dimensi...  87.7 us
    all_to_all x1, waiting for transfers between devices, per_device(): lax.all_to_all(grouped, 'col', split_axis=1, concat_axis=0, tiled=True)  44.1 us
    dot_general x1, matrix products, per_device(): lax.dot_general(row_block, sign_block, (((1,), (1,)), ((), ())), precisio...  37.1 us
    all_gather x1, waiting for transfers between devices, per_device(): row_block = lax.all_gather(new_momentum, 'col', axis=0, tiled=True)  20.3 us
    reshape x2, local copies, waits for them, and re-layouts, per_device(): grouped = out_grad.reshape(quarter_rows, data_count, col_count, owner_rows)  12.7 us
    reduce_scatter x1, waiting for transfers between devices, per_device(): lax.psum_scatter(partial_sketch, 'col', scatter_dimension=0, tiled=True)  12.6 us
    dot_general x1, matrix products, per_device(): jnp.dot(tokens, sign_block.astype(jnp.bfloat16), preferred_element_type=j...  7.71 us
    reshape x1, local copies, waits for them, and re-layouts, per_device(): jnp.transpose(grouped, (0, 2, 1, 3))  7.37 us
  transfers between devices with their start and end apart: 5, of which 4 were waited for; matrix products, arithmetic and copies ran while one was open for 9% of the time, Pallas kernels for 0%

commit v1 on v0

--- a/solution.py
+++ b/solution.py
@@ -53,7 +53,12 @@
     )
     projected = projected / jnp.float32(total_tokens)
     new_momentum = 0.8 * momentum + 0.2 * projected
-    row_block = lax.all_gather(new_momentum, "col", axis=0, tiled=True)
+    ring = [new_momentum]
+    for hop in range(3):
+        ring.append(lax.ppermute(ring[-1], "col", [(dev, (dev + 1) % 4) for dev in range(4)]))
+    row_block = jnp.roll(
+        jnp.concatenate(ring[::-1], axis=0), (lax.axis_index("col") + 1) * ring[0].shape[0], axis=0
+    )
     dense_grad = (
         lax.dot_general(
             row_block,

time: 264 us -> 267 us (1.011)
  waiting for transfers between devices: 165 us -> 169 us
    ppermute x0 -> x3, waiting for transfers between devices: none -> 24.8 us  [per_device(): lax.ppermute(ring[-1], 'col', [(dev, (dev + 1) % 4) for dev in range(4)])]
    all_gather x1 -> x0, waiting for transfers between devices: 20.3 us -> none  [per_device(): row_block = lax.all_gather(new_momentum, 'col', axis=0, tiled=True)]
  transfers between devices with their start and end apart: 5 -> 7, of which waited for: 4 -> 6; matrix products, arithmetic and copies ran while one was open for 9% -> 9% of each run, Pallas kernels for 0% -> 0%
where the time goes in v1:
time: 267 us; the launch traced here: 266 us
  waiting for transfers between devices  169 us (63%)
  matrix products  51 us (19%)
  local copies, waits for them, and re-layouts  22.8 us (9%)
  between operations  15.1 us (6%)
  starting transfers between devices  5.03 us (2%)
  other arithmetic  2.9 us (1%)
    reduce_scatter x1, waiting for transfers between devices, per_device(): lax.psum_scatter(contract(regrouped, shard_sketch), 'dp', scatter_dimensi...  87.7 us
    all_to_all x1, waiting for transfers between devices, per_device(): lax.all_to_all(grouped, 'col', split_axis=1, concat_axis=0, tiled=True)  44.1 us
    dot_general x1, matrix products, per_device(): lax.dot_general(row_block, sign_block, (((1,), (1,)), ((), ())), precisio...  36.5 us
    ppermute x3, waiting for transfers between devices, per_device(): lax.ppermute(ring[-1], 'col', [(dev, (dev + 1) % 4) for dev in range(4)])  24.8 us
    reshape x2, local copies, waits for them, and re-layouts, per_device(): grouped = out_grad.reshape(quarter_rows, data_count, col_count, owner_rows)  12.7 us
    reduce_scatter x1, waiting for transfers between devices, per_device(): lax.psum_scatter(partial_sketch, 'col', scatter_dimension=0, tiled=True)  12.6 us
    dot_general x1, matrix products, per_device(): jnp.dot(tokens, sign_block.astype(jnp.bfloat16), preferred_element_type=j...  7.71 us
    reshape x1, local copies, waits for them, and re-layouts, per_device(): jnp.transpose(grouped, (0, 2, 1, 3))  7.37 us
  transfers between devices with their start and end apart: 7, of which 6 were waited for; matrix products, arithmetic and copies ran while one was open for 9% of the time, Pallas kernels for 0%

profile of v1, /device:TPU:0, one launch (start us, length us, event | category | flops | bytes accessed | tf_op | source)
XLA Modules:
  0.0 266.1 jit_solution(16783042498085096468)
XLA Ops:
  7.2 0.0 reduce-scatter.3.cloned.1.call-start
  8.5 7.7 %multiply_bitcast_fusion = f32[1024,512]{0,1:T(8,128)} fusion(bf16[1024,2048]{1,0:T(8,128)(2,1)} %param.7, s32[]{:T(128)} %bitcast.1, s32[]{:T(128)} %bitcast, s32[2048]{0:T(1024)S(1)} %add_multiply_fusion), kind=kOutput, calls=%fused_computation.10 | convolution fusion | flops 2170028032 | bytes 6299656 | tf_op jit(solution)/shard_map/dot_general | solution.py:35
  16.2 0.0 reduce-scatter.3.cloned.1.call-update
  16.3 7.8 %reshape.26 = bf16[256,8,4,256]{3,2,1,0:T(4,128)(2,1)} reshape(bf16[256,8192]{1,0:T(8,128)(2,1)} %param.8) | data formatting | bytes 8388608 | tf_op jit(solution)/shard_map/reshape | solution.py:44
  24.1 4.9 %copy.16 = bf16[256,8,4,256]{3,1,0,2:T(8,128)(2,1)} copy(bf16[256,8,4,256]{3,2,1,0:T(4,128)(2,1)} %reshape.26) | data formatting | bytes 8388608 | tf_op jit(solution)/shard_map/reshape | solution.py:44
  29.0 7.4 %reshape.27 = bf16[256,4,2048]{2,0,1:T(8,128)(2,1)} reshape(bf16[256,4,8,256]{3,2,0,1:T(8,128)(2,1)} %bitcast.21) | data formatting | bytes 8388608 | tf_op jit(solution)/shard_map/reshape | solution.py:45
  36.3 4.8 %all-to-all-start = ((bf16[256,4,2048]{2,0,1:T(8,128)(2,1)}), bf16[256,4,2048]{2,0,1:T(8,128)(2,1)}, u32[]{:S(2)}, u32[]{:S(2)}) async-start(bf16[256,4,2048]{2,0,1:T(8,128)(2,1)} %reshape.27), calls=%async_computation.1 | async-start | bytes 8388608 | tf_op jit(solution)/shard_map/all_to_all | solution.py:48
  41.2 0.0 all-gather.2.cloned.1.call-start
  41.2 12.6 %reduce-scatter.3.cloned.1.call-done = f32[256,512]{0,1:T(8,128)} async-done(((f32[1024,512]{0,1:T(8,128)}), f32[256,512]{0,1:T(8,128)}) %reduce-scatter.3.cloned.1.call-update) | async-done | bytes 524304 | tf_op jit(solution)/shard_map/reduce_scatter | solution.py:38
  53.8 1.8 convert_element_type.11
  55.6 0.0 all-gather.2.cloned.1.call-update
  55.6 0.0 reduce-scatter.5.cloned.1.call-start
  55.7 44.1 %all-to-all-done = bf16[256,4,2048]{2,0,1:T(8,128)(2,1)} async-done(((bf16[256,4,2048]{2,0,1:T(8,128)(2,1)}), bf16[256,4,2048]{2,0,1:T(8,128)(2,1)}, u32[]{:S(2)}, u32[]{:S(2)}) %all-to-all-start) | async-done | bytes 4194336 | tf_op jit(solution)/shard_map/all_to_all | solution.py:48
  99.7 0.0 all-gather.2.cloned.1.call-done
  99.7 6.9 %convolution_bitcast_fusion = f32[2048,512]{0,1:T(8,128)} fusion(bf16[1024,512]{0,1:T(8,128)(2,1)} %all-gather.2.cloned.1.call-done, bf16[1024,2048]{1,0:T(8,128)(2,1)} %bitcast.6), kind=kOutput, calls=%fused_computation.7 | convolution fusion | flops 2147483648 | bytes 9437184 | tf_op jit(solution)/shard_map/dot_general | solution.py:22
  106.6 0.0 copy-start
  106.6 0.0 reduce-scatter.5.cloned.1.call-update
  106.6 1.0 copy-done
  107.6 0.2 copy.12
  107.8 87.7 %reduce-scatter.5.cloned.1.call-done = f32[256,512]{0,1:T(8,128)} async-done(((f32[2048,512]{0,1:T(8,128)}), f32[256,512]{0,1:T(8,128)}) %reduce-scatter.5.cloned.1.call-update) | async-done | bytes 524304 | tf_op jit(solution)/shard_map/reduce_scatter | solution.py:51
  195.5 1.1 multiply_add_fusion.1
  196.7 0.1 collective-permute-start
  196.7 8.6 %collective-permute-done = f32[256,512]{0,1:T(8,128)S(1)} collective-permute-done((f32[256,512]{0,1:T(8,128)S(1)}, f32[256,512]{0,1:T(8,128)S(1)}, u32[]{:S(2)}, u32[]{:S(2)}) %collective-permute-start) | collective-permute-done | bytes 524320 | tf_op jit(solution)/shard_map/ppermute | solution.py:58
  205.3 0.0 collective-permute-start.1
  205.3 8.6 %collective-permute-done.1 = f32[256,512]{0,1:T(8,128)S(1)} collective-permute-done((f32[256,512]{0,1:T(8,128)S(1)}, f32[256,512]{0,1:T(8,128)S(1)}, u32[]{:S(2)}, u32[]{:S(2)}) %collective-permute-start.1) | collective-permute-done | bytes 524320 | tf_op jit(solution)/shard_map/ppermute | solution.py:58
  213.9 0.0 collective-permute-start.2
  213.9 1.0 copy.14
  214.9 7.6 %collective-permute-done.2 = f32[256,512]{0,1:T(8,128)S(1)} collective-permute-done((f32[256,512]{0,1:T(8,128)S(1)}, f32[256,512]{0,1:T(8,128)S(1)}, u32[]{:S(2)}, u32[]{:S(2)}) %collective-permute-start.2) | collective-permute-done | bytes 524320 | tf_op jit(solution)/shard_map/ppermute | solution.py:58
  222.5 0.1 constant_dynamic-update-slice_fusion.7
  222.6 0.1 constant_dynamic-update-slice_fusion.6
  222.7 0.1 constant_dynamic-update-slice_fusion.5
  222.8 0.1 constant_dynamic-update-slice_fusion.4
  222.8 0.1 constant_dynamic-update-slice_fusion.3
  222.9 0.1 constant_dynamic-update-slice_fusion.2
  223.0 0.1 constant_dynamic-update-slice_fusion.1
  223.1 0.1 constant_dynamic-update-slice_fusion
  223.2 36.5 %divide_subtract_fusion = (f32[1024,2048]{1,0:T(8,128)}, f32[1024,2048]{1,0:T(8,128)}) fusion(f32[1024,2048]{1,0:T(8,128)} %param.9, f32[1024,2048]{1,0:T(8,128)} %param.10, s32[]{:T(128)} %bitcast.1, s32[]{:T(128)} %bitcast, s32[2048]{0:T(1024)S(1)} %add_multiply_fusion, f32[2048,512]{0,1:T(8,128)S(1)} %constant_dynamic-update-slice_fusion, s32[]{:T(128)S(6)} %select_n.14), kind=kOutput, calls=%fused_computation | convolution fusion | flops 12924747776 | bytes 35659788 | tf_op jit(solution)/shard_map/dot_general | solution.py:63
  (1 shorter events, 0.0 us)
Async XLA Ops:
  7.2 46.7 %reduce-scatter.3.cloned.1.call-start = ((), (), s32[]{:S(2)}) async-start(), calls=%async_computation.3 | async-start | bytes 2621440 | tf_op jit(solution)/shard_map/reduce_scatter | solution.py:38
  36.3 63.4 %all-to-all-start = ((bf16[256,4,2048]{2,0,1:T(8,128)(2,1)}), bf16[256,4,2048]{2,0,1:T(8,128)(2,1)}, u32[]{:S(2)}, u32[]{:S(2)}) async-start(bf16[256,4,2048]{2,0,1:T(8,128)(2,1)} %reshape.27), calls=%async_computation.1 | async-start | bytes 8388608 | tf_op jit(solution)/shard_map/all_to_all | solution.py:48
  41.2 58.5 %all-gather.2.cloned.1.call-start = ((), (), s32[]{:S(2)}) async-start(), calls=%async_computation.4 | async-start | bytes 1310720 | tf_op jit(solution)/shard_map/all_gather | solution.py:50
  55.6 139.9 %reduce-scatter.5.cloned.1.call-start = ((), (), s32[]{:S(2)}) async-start(), calls=%async_computation.5 | async-start | bytes 4718592 | tf_op jit(solution)/shard_map/reduce_scatter | solution.py:51
  106.6 1.0 copy-start
  196.7 8.7 %collective-permute-start = (f32[256,512]{0,1:T(8,128)S(1)}, f32[256,512]{0,1:T(8,128)S(1)}, u32[]{:S(2)}, u32[]{:S(2)}) collective-permute-start(f32[256,512]{0,1:T(8,128)S(1)} %multiply_add_fusion.1), channel_id=1, source_target_pairs={{0,1},{1,2},{2,3},{3,0},{4,5},{5,6},{6,7},{7,4},{8,9},{9,10},{10,1... | collective-permute-start | bytes 1572872 | tf_op jit(solution)/shard_map/ppermute | solution.py:58
  205.3 8.6 %collective-permute-start.1 = (f32[256,512]{0,1:T(8,128)S(1)}, f32[256,512]{0,1:T(8,128)S(1)}, u32[]{:S(2)}, u32[]{:S(2)}) collective-permute-start(f32[256,512]{0,1:T(8,128)S(1)} %collective-permute-done), channel_id=1, source_target_pairs={{0,1},{1,2},{2,3},{3,0},{4,5},{5,6},{6,7},{7,4},{8,9},{9,10},{10,1... | collective-permute-start | bytes 1572872 | tf_op jit(solution)/shard_map/ppermute | solution.py:58
  213.9 8.6 %collective-permute-start.2 = (f32[256,512]{0,1:T(8,128)S(1)}, f32[256,512]{0,1:T(8,128)S(1)}, u32[]{:S(2)}, u32[]{:S(2)}) collective-permute-start(f32[256,512]{0,1:T(8,128)S(1)} %collective-permute-done.1), channel_id=1, source_target_pairs={{0,1},{1,2},{2,3},{3,0},{4,5},{5,6},{6,7},{7,4},{8,9},{9,10},{10,1... | collective-permute-start | bytes 1572872 | tf_op jit(solution)/shard_map/ppermute | solution.py:58
Sparse Core Ops, SparseCore 0:
  16.4 37.4 reduce-scatter.2
  56.0 21.9 all-gather.1
  106.7 88.7 reduce-scatter.4
